TPU v7x, 256 devices: a whole 4x4x8 slice. The times are simulated.
256 devices in a mesh: dp: 4 (over x), ctx: 64 (over z, y, core).
Axes of the slice: x: 4, y: 4, z: 8, core: 2. Of those that a mesh axis runs over, the one named last changes fastest.
Arguments:
- queries: bfloat16 [2, 32768, 2048], P(None, ('dp', 'ctx')), may hold values from -6 to 6
- keys: bfloat16 [2, 32768, 1024], P(None, ('dp', 'ctx')), may hold values from -6 to 6
- values: bfloat16 [2, 32768, 1024], P(None, ('dp', 'ctx')), may hold values from -6 to 6
- doc_start: int32 [2, 32768], P(None, ('dp', 'ctx')), may hold values from 0 to 16383, as said below
- gain_q: float32 [128], replicated, may hold values from 0.5 to 1.5
- key_norm_gain: float32 [128], replicated, may hold values from 0.5 to 1.5
- cotangent: bfloat16 [2, 32768, 2048], P(None, ('dp', 'ctx')), may hold values from -6 to 6
Outputs:
- attended: bfloat16 [2, 32768, 2048], P(None, ('dp', 'ctx'))
- grad_queries: bfloat16 [2, 32768, 2048], P(None, ('dp', 'ctx'))
- grad_keys: bfloat16 [2, 32768, 1024], P(None, ('dp', 'ctx'))
- value_gradients: bfloat16 [2, 32768, 1024], P(None, ('dp', 'ctx'))
- grad_gain_q: float32 [128], replicated
- grad_gain_k: float32 [128], replicated
Inputs may be any that keep to these rules, and one draw needn't show every extreme that they name: doc_start gives each token the position in its sequence of its document's first token; the documents of a sequence are runs of 1 to 256 tokens, the first starting at 0, and every sequence has one of exactly 256 tokens.
All inputs are finite; a program needn't handle non-finite values.
Results may differ from a plain program's by a relative error of at most 0.012.
Values may be sent and summed in bfloat16 or wider, within the bound.
No kernel may reach another device: no remote copies, remote signals or barrier semaphores. Data moves between devices by JAX's collectives and lax.ppermute only.
A program may use at most 128 MiB of HBM per device.

v0:
```python
from functools import partial
import jax
import jax.numpy as jnp
from jax import lax
from jax.sharding import PartitionSpec as P

REACH = 2
query_factor = 168.0 ** (-0.5)
rotary_base = 1000000.0
norm_epsilon = 1e-06


def from_behind(block, axis, distance):
    devices = range(lax.axis_size(axis))
    route = [(i - distance, i) for i in devices if i - distance in devices]
    return lax.ppermute(block, axis, route)


def rotary_angles(position, head_width):
    exponent = jnp.arange(head_width // 2, dtype=jnp.float32) * (2.0 / head_width)
    frequency = jnp.exp(-exponent * jnp.log(jnp.float32(rotary_base)))
    return position.astype(jnp.float32)[..., None] * frequency


def prepare(tensor, gain, angle, factor):
    inverse = lax.rsqrt(jnp.mean(tensor * tensor, axis=-1, keepdims=True) + norm_epsilon)
    normed = tensor * inverse * gain
    middle = tensor.shape[-1] // 2
    cosine = jnp.cos(angle)[..., None, :]
    sine = jnp.sin(angle)[..., None, :]
    first = normed[..., :middle]
    second = normed[..., middle:]
    return (
        jnp.concatenate([first * cosine - second * sine, second * cosine + first * sine], axis=-1)
        * factor
    )


def slot_positions(slot, rows, group, block):
    ascending = slot * block + rows
    descending = slot * block + block - 1 - rows
    inside = (slot >= 0) & (slot < 2 * group)
    return jnp.where(inside, jnp.where(slot < group, ascending, descending), -1)


def visible(doc_query, query_position, key_position):
    return (doc_query[:, :, None] <= key_position[:, None, :]) & (
        key_position[:, None, :] <= query_position[:, :, None]
    )


def forward_terms(q_rot, key_panel, value_panel, mask):
    scores = jnp.einsum("xihrd,xjhd->xhrij", q_rot, key_panel, preferred_element_type=jnp.float32)
    weights = jnp.where(mask[:, None, None], jnp.exp(scores), 0.0)
    summed = jnp.sum(weights, axis=-1)
    mixed = jnp.einsum(
        "xhrij,xjhd->xihrd",
        weights.astype(jnp.bfloat16),
        value_panel,
        preferred_element_type=jnp.float32,
    )
    return (summed, mixed)


def softmax_grads(q_rot, cotangent_heads, key_panel, value_panel, mask, total, delta):
    scores = jnp.einsum("xihrd,xjhd->xhrij", q_rot, key_panel, preferred_element_type=jnp.float32)
    probs = jnp.where(mask[:, None, None], jnp.exp(scores) / total[..., None], 0.0)
    dprob = jnp.einsum(
        "xihrd,xjhd->xhrij", cotangent_heads, value_panel, preferred_element_type=jnp.float32
    )
    dscore = probs * (dprob - delta[..., None])
    return (probs.astype(jnp.bfloat16), dscore.astype(jnp.bfloat16))


def key_grads(probs, dscore, q_rot, cotangent_heads):
    grad_key = jnp.einsum("xhrij,xihrd->xjhd", dscore, q_rot, preferred_element_type=jnp.float32)
    grad_value = jnp.einsum(
        "xhrij,xihrd->xjhd", probs, cotangent_heads, preferred_element_type=jnp.float32
    )
    return (grad_key, grad_value)


def all_grads(q_rot, cotangent_heads, key_panel, value_panel, mask, total, delta):
    probs, dscore = softmax_grads(
        q_rot, cotangent_heads, key_panel, value_panel, mask, total, delta
    )
    grad_key, grad_value = key_grads(probs, dscore, q_rot, cotangent_heads)
    grad_query = jnp.einsum(
        "xhrij,xjhd->xihrd", dscore, key_panel, preferred_element_type=jnp.float32
    )
    return (grad_query, grad_key, grad_value)


def advance(lower, upper, at_fold):
    moved_lower = from_behind(lower, "ctx", 1)
    moved_upper = from_behind(upper, "ctx", -1)
    return (moved_lower, jnp.where(at_fold, lower, moved_upper))


def retreat_grads(lower, upper, at_fold, at_start):
    moved_lower = from_behind(lower, "ctx", -1)
    moved_upper = from_behind(upper, "ctx", 1)
    return (jnp.where(at_fold, upper, moved_lower), jnp.where(at_start, 0.0, moved_upper))


def shards(queries, keys, values, doc_start, gain_q, key_norm_gain, cotangent):
    group = lax.axis_size("ctx")
    block = queries.shape[1]
    head_width = gain_q.shape[0]
    q_heads = queries.shape[2] // head_width
    kv_heads = keys.shape[2] // head_width
    repeat = q_heads // kv_heads
    group_index = lax.axis_index("ctx")
    at_fold = group_index == group - 1
    at_start = group_index == 0
    rows = jnp.arange(block, dtype=jnp.int32)[None, :]
    own_slot = jnp.stack([group_index, 2 * group - 1 - group_index])[:, None]
    own_position = slot_positions(own_slot, rows, group, block)
    angle = rotary_angles(own_position, head_width)
    q_rotated, q_back = jax.vjp(
        lambda tensor, gain: prepare(tensor, gain, angle, query_factor),
        queries.astype(jnp.float32).reshape(2, block, q_heads, head_width),
        gain_q,
    )
    q_rot = q_rotated.astype(jnp.bfloat16).reshape(2, block, kv_heads, repeat, head_width)
    k_rotated, k_back = jax.vjp(
        lambda tensor, gain: prepare(tensor, gain, angle, 1.0),
        keys.astype(jnp.float32).reshape(2, block, kv_heads, head_width),
        key_norm_gain,
    )
    k_rot = k_rotated.astype(jnp.bfloat16)
    cotangent_heads = cotangent.reshape(2, block, kv_heads, repeat, head_width)
    local_key_panel = jnp.stack([k_rot.reshape(2, block, -1), values], axis=1)
    panels = [local_key_panel]
    lower, upper = (local_key_panel[0], local_key_panel[1])
    for step in range(REACH):
        lower, upper = advance(lower, upper, at_fold)
        panels.append(jnp.stack([lower, upper]))
    masks = [
        visible(doc_start, own_position, slot_positions(own_slot - step, rows, group, block))
        for step in range(REACH + 1)
    ]
    zeros_q = jnp.zeros((2, block, kv_heads, repeat, head_width), jnp.float32)
    summed = jnp.zeros((2, kv_heads, repeat, block), jnp.float32)
    mixed = zeros_q
    key_panels = []
    value_panels = []
    for step in range(REACH + 1):
        key_panel = panels[step][:, 0].reshape(2, block, kv_heads, head_width)
        value_panel = panels[step][:, 1].reshape(2, block, kv_heads, head_width)
        key_panels.append(key_panel)
        value_panels.append(value_panel)
        compute = partial(forward_terms, q_rot, key_panel, value_panel, masks[step])
        if step == 0:
            terms = compute()
        else:
            terms = compute()
        summed = summed + terms[0]
        mixed = mixed + terms[1]
    attended_heads = (mixed / jnp.transpose(summed, (0, 3, 1, 2))[..., None]).astype(jnp.bfloat16)
    delta = jnp.einsum(
        "xihrd,xihrd->xhri", cotangent_heads, attended_heads, preferred_element_type=jnp.float32
    )
    grad_q_heads = zeros_q
    for step in range(REACH, -1, -1):
        compute = partial(
            all_grads,
            q_rot,
            cotangent_heads,
            key_panels[step],
            value_panels[step],
            masks[step],
            summed,
            delta,
        )
        if step == 0:
            terms = compute()
        else:
            terms = compute()
        grad_q_heads = grad_q_heads + terms[0]
        contribution = jnp.stack(
            [terms[1].reshape(2, block, -1), terms[2].reshape(2, block, -1)], axis=1
        )
        if step == REACH:
            carried_lower, carried_upper = (contribution[0], contribution[1])
        else:
            carried_lower, carried_upper = retreat_grads(
                carried_lower, carried_upper, at_fold, at_start
            )
            carried_lower = carried_lower + contribution[0]
            carried_upper = carried_upper + contribution[1]
    key_value_gradient = jnp.stack([carried_lower, carried_upper])
    grad_k_heads = key_value_gradient[:, 0].reshape(2, block, kv_heads, head_width)
    grad_v_flat = key_value_gradient[:, 1]
    grad_queries, grad_gain_q = q_back(grad_q_heads.reshape(2, block, q_heads, head_width))
    grad_keys, grad_gain_k = k_back(grad_k_heads)
    grad_gain_q, grad_gain_k = lax.psum((grad_gain_q, grad_gain_k), ("dp", "ctx"))
    return (
        attended_heads.reshape(2, block, -1),
        grad_queries.reshape(2, block, -1).astype(jnp.bfloat16),
        grad_keys.reshape(2, block, -1).astype(jnp.bfloat16),
        grad_v_flat.astype(jnp.bfloat16),
        grad_gain_q,
        grad_gain_k,
    )


def solution(mesh):
    placed = (
        P(None, ("dp", "ctx"), None),
        P(None, ("dp", "ctx"), None),
        P(None, ("dp", "ctx"), None),
        P(None, ("dp", "ctx")),
        P(),
        P(),
        P(None, ("dp", "ctx"), None),
    )
    return jax.shard_map(
        shards,
        mesh=mesh,
        in_specs=placed,
        out_specs=(
            P(None, ("dp", "ctx"), None),
            P(None, ("dp", "ctx"), None),
            P(None, ("dp", "ctx"), None),
            P(None, ("dp", "ctx"), None),
            P(),
            P(),
        ),
        check_vma=False,
    )
```

profile of v0, /device:TPU:1, one launch (start us, length us, event | category | flops | bytes accessed | tf_op | source)
XLA Modules:
  0.0 234.9 jit_solution(2773730723189249938)
XLA Ops:
  0.6 0.6 broadcast_multiply_fusion.1
  2.4 1.3 copy.215
  4.1 0.7 fusion.83
  7.5 0.9 fusion.65
  8.4 5.1 %collective-permute-start.1 = (bf16[2,128,1024]{1,2,0:T(8,128)(2,1)}, bf16[2,128,1024]{1,2,0:T(8,128)(2,1)}, u32[]{:S(2)}, u32[]{:S(2)}) collective-permute-start(bf16[2,128,1024]{1,2,0:T(8,128)(2,1)} %fusion.65), channel_id=1, source_target_pairs={{1,0},{2,1},{3,2},{4,3},{5,4},{6,5},{7,6},{8,7},{9,8},{10,9},{11,1... | collective-permute-start | bytes 1572872 | tf_op jit(solution)/shard_map/ppermute | solution.py:16
  13.6 1.5 copy.330
  15.9 0.7 fusion.21
  16.6 0.7 multiply_subtract_fusion
  17.4 2.0 copy.219
  19.3 1.9 copy.220
  21.5 2.9 %fusion.3 = bf16[2,128,8,2,128]{4,1,3,2,0:T(8,128)(2,1)S(1)} fusion(f32[2,128,8,2,64]{4,1,3,2,0:T(8,128)} %bitcast.308, f32[2,128,8,2,64]{4,1,3,2,0:T(8,128)} %bitcast.307), kind=kLoop, calls=%fused_computation.9 | loop fusion | flops 1572864 | bytes 3145728 | tf_op jit(solution)/shard_map/convert_element_type | solution.py:125
  24.6 0.8 compare_and_fusion.2
  25.4 2.1 broadcast_select_fusion
  27.5 1.9 collective-permute-start
  29.4 2.4 %fusion.15 = (f32[2,8,2,128]{3,2,1,0:T(2,128)}, f32[2,8,128,128,2]{3,2,4,1,0:T(8,128)}) fusion(pred[2,128,128]{1,2,0:T(8,128)(4,1)S(1)} %get-tuple-element.68, bf16[2,128,8,2,128]{4,1,3,2,0:T(8,128)(2,1)S(1)} %fusion.3, bf16[2,128,8,128]{3,1,2,0:T(8,128)(2,1)S(1)} %copy-done.9), kind=kOutput, calls=%fused_computation.48 | convolution fusion | flops 135262208 | bytes 3719168 | tf_op jit(solution)/shard_map/xihrd,xjhd->xhrij/dot_general | solution.py:53
  31.8 3.2 %collective-permute-start.3 = (bf16[2,128,1024]{1,2,0:T(8,128)(2,1)}, bf16[2,128,1024]{1,2,0:T(8,128)(2,1)}, u32[]{:S(2)}, u32[]{:S(2)}) collective-permute-start(bf16[2,128,1024]{1,2,0:T(8,128)(2,1)} %get-tuple-element.48), channel_id=1, source_target_pairs={{1,0},{2,1},{3,2},{4,3},{5,4},{6,5},{7,6},{8,7},{9,8},{10,9},{11,1... | collective-permute-start | bytes 1572872 | tf_op jit(solution)/shard_map/ppermute | solution.py:16
  35.0 0.8 bitcast_bitcast_fusion
  35.9 2.6 %reshape.655 = bf16[2,128,8,2,128]{4,3,2,1,0:T(2,128)(2,1)} reshape(bf16[2,128,2048]{2,1,0:T(8,128)(2,1)} %param.13) | data formatting | bytes 2097152 | tf_op jit(solution)/shard_map/reshape | solution.py:132
  38.4 3.7 %copy.247 = bf16[2,128,8,2,128]{1,4,3,2,0:T(8,128)(2,1)} copy(bf16[2,128,8,2,128]{4,3,2,1,0:T(2,128)(2,1)} %reshape.655) | data formatting | bytes 2097152 | tf_op jit(solution)/shard_map/reshape | solution.py:132
  42.1 2.7 %collective-permute-start.2 = (bf16[2,128,1024]{1,2,0:T(8,128)(2,1)}, bf16[2,128,1024]{1,2,0:T(8,128)(2,1)S(1)}, u32[]{:S(2)}, u32[]{:S(2)}) collective-permute-start(bf16[2,128,1024]{1,2,0:T(8,128)(2,1)} %collective-permute-done), channel_id=1, source_target_pairs={{0,1},{1,2},{2,3},{3,4},{4,5},{5,6},{6,7},{7,8},{8,9},{9,10},{10,1... | collective-permute-start | bytes 1572872 | tf_op jit(solution)/shard_map/ppermute | solution.py:16
  44.8 1.3 pad_maximum_fusion.5
  46.7 1.5 select_bitcast_fusion
  48.7 2.3 collective-permute-done.2
  52.3 0.8 copy-done.13
  53.1 1.0 copy-done.29
  54.2 2.4 %bitcast_convert_fusion = (f32[2,8,2,128,128]{3,4,2,1,0:T(8,128)}, bf16[2,128,8,2,128]{1,4,3,2,0:T(8,128)(2,1)}) fusion(f32[2,128,8,2]{1,3,2,0:T(2,128)S(1)} %bitcast.339, f32[2,8,128,2,128]{4,2,3,1,0:T(8,128)S(1)} %fusion.23, f32[2,8,128,2,128]{4,2,3,1,0:T(8,128)S(1)} %fusion.25, f32[2,8,128,128,2]{3,2,4,1,0:T(8,128)S(1)} %copy-done.29, ...), kind=kOutput, calls=%fused_computation.87 | convolution fusion | flops 137887744 | bytes 10010624 | tf_op jit(solution)/shard_map/xhrij,xjhd->xihrd/dot_general | solution.py:56
  56.6 4.2 %copy.285 = f32[2,8,2,128,128]{4,2,1,3,0:T(2,128)} copy(f32[2,8,2,128,128]{3,4,2,1,0:T(8,128)} %get-tuple-element.90) | data formatting | bytes 4194304
  60.8 5.1 %multiply_reduce_fusion = f32[2,8,2,128]{2,1,3,0:T(8,128)} fusion(f32[2,8,2,128,128]{4,2,1,3,0:T(2,128)} %copy.285, bf16[2,128,8,2,128]{4,3,2,1,0:T(2,128)(2,1)} %reshape.655), kind=kLoop, calls=%fused_computation.40 | loop fusion | flops 1568768 | bytes 3162112
  65.9 2.2 copy.286
  68.1 2.5 %fusion.49 = f32[2,8,128,128,1]{2,3,4,1,0:T(8,128)S(1)} fusion(bf16[2,128,8,2,128]{1,4,3,2,0:T(8,128)(2,1)} %copy.247, f32[2,8,128,128,2]{3,2,4,1,0:T(8,128)} %copy-done.13, f32[2,8,2,128]{3,2,1,0:T(2,128)} %bitcast.340, pred[2,128,128]{1,2,0:T(8,128)(4,1)} %get-tuple-element.69), kind=kOutput, calls=%fused_computation.97 | convolution fusion | flops 135790592 | bytes 4243456 | tf_op jit(solution)/shard_map/xhrij,xihrd->xjhd/dot_general | solution.py:77
  71.1 0.8 fusion.9
  71.8 0.8 copy-done.12
  72.7 0.8 fusion.7
  73.5 0.8 copy-done.30
  74.4 0.7 fusion.5
  75.7 2.1 collective-permute-start.5
  80.8 11.8 %collective-permute-done.5 = f32[2,128,1024]{1,2,0:T(8,128)S(1)} collective-permute-done((f32[2,128,1024]{1,2,0:T(8,128)S(1)}, f32[2,128,1024]{1,2,0:T(8,128)S(1)}, u32[]{:S(2)}, u32[]{:S(2)}) %collective-permute-start.5) | collective-permute-done | bytes 1048608 | tf_op jit(solution)/shard_map/ppermute | solution.py:16
  92.6 1.5 fusion.43
  94.1 1.9 collective-permute-start.4
  96.0 3.6 %collective-permute-start.6 = (f32[2,128,1024]{1,2,0:T(8,128)}, f32[2,128,1024]{1,2,0:T(8,128)}, u32[]{:S(2)}, u32[]{:S(2)}) collective-permute-start(f32[2,128,1024]{1,2,0:T(8,128)} %get-tuple-element.44), channel_id=1, source_target_pairs={{1,0},{2,1},{3,2},{4,3},{5,4},{6,5},{7,6},{8,7},{9,8},{10,9},{11,1... | collective-permute-start | bytes 3145736 | tf_op jit(solution)/shard_map/ppermute | solution.py:16
  99.6 1.5 fusion.84
  101.1 3.3 %copy.325 = f32[2,128,16,64]{3,2,1,0:T(8,128)} copy(f32[2,128,16,64]{1,3,2,0:T(8,128)} %get-tuple-element.58) | data formatting | bytes 2097152
  104.4 3.3 %copy.326 = f32[2,128,16,64]{3,2,1,0:T(8,128)} copy(f32[2,128,16,64]{1,3,2,0:T(8,128)} %get-tuple-element.59) | data formatting | bytes 2097152
  107.7 1.9 fusion.89
  109.8 1.5 fusion.45
  111.4 1.1 collective-permute-done.6
  112.5 3.0 %fusion.32 = (f32[1,2,128,1024]{2,3,1,0:T(8,128)S(1)}, f32[2,128,1024]{1,2,0:T(8,128)}) fusion(f32[2,1,128,1024]{2,3,1,0:T(8,128)S(1)} %bitcast.301, f32[2,1,128,1024]{2,3,1,0:T(8,128)S(1)} %bitcast.319, f32[2,128,1024]{1,2,0:T(8,128)} %collective-permute-done.6, pred[]{:T(512)S(6)} %eq.6, f32[2,1,128,1024]{2,3,1,0:T(8,128)S(1)} %bitcast.323, ...), kind=kLoop, calls=%fused_computation.63 | loop fusion | flops 1572864 | bytes 8388610 | tf_op jit(solution)/shard_map/stack | solution.py:192
  115.5 2.0 collective-permute-start.7
  118.2 2.5 %multiply_reduce_fusion.1 = (f32[128]{0:T(128)}, f32[2,128,16]{2,1,0:T(8,128)}) fusion(f32[2,128,16]{2,1,0:T(8,128)S(1)} %copy.218, f32[2,128,16,64]{3,2,1,0:T(8,128)S(1)} %get-tuple-element.53, f32[2,128,16,64]{3,2,1,0:T(8,128)S(1)} %get-tuple-element.52, f32[128]{0:T(128)S(1)} %copy-done.60, f32[2,128,16,128]{3,2,1,0:T(8,128)S(1)} %bitcast.299), kind=kLoop, calls=%fused_computation.41 | loop fusion | flops 3665792 | bytes 4228096 | tf_op jit(solution)/shard_map/transpose(jvp())/reduce_sum | solution.py:27
  120.7 1.6 copy.242
  122.3 1.3 multiply_multiply_fusion.1
  123.6 1.5 copy.243
  125.1 4.8 %fusion = bf16[2,128,16,128]{3,2,1,0:T(8,128)(2,1)} fusion(f32[2,128,16]{2,1,0:T(8,128)} %copy.243, f32[128]{0:T(128)} %param.11, f32[2,128,16]{2,1,0:T(8,128)S(1)} %copy.218, f32[2,128,16,64]{3,2,1,0:T(8,128)} %copy-done.1, f32[2,128,16,64]{3,2,1,0:T(8,128)} %copy-done, f32[2,128,16,128]{3,2,1,0:T(8,128)S(1)} %bitcast.300), kind=kLoop, calls=%fused_computation.1 | loop fusion | flops 3670016 | bytes 5276160 | tf_op jit(solution)/shard_map/convert_element_type | solution.py:200
  129.9 2.4 %convert_element_type.84 = bf16[2,128,2048]{2,1,0:T(8,128)(2,1)} reshape(bf16[2,128,16,128]{3,2,1,0:T(8,128)(2,1)} %fusion) | data formatting | bytes 2097152 | tf_op jit(solution)/shard_map/convert_element_type | solution.py:200
  132.4 1.3 copy.267
  133.7 1.5 fusion.41
  135.3 0.9 fusion.64
  136.6 1.4 copy.328
  138.0 1.0 copy.269
  139.0 1.6 multiply_add_fusion.4
  140.6 0.9 multiply_reduce_fusion.2
  141.5 1.0 fusion.22
  142.8 1.0 copy.268
  143.9 91.0 %all-reduce.4 = (f32[128]{0:T(128)}, f32[128]{0:T(128)}) all-reduce(f32[128]{0:T(128)S(1)} %copy-done.72, f32[128]{0:T(128)S(1)} %get-tuple-element.38), channel_id=1, replica_groups=mesh['dp'=4,'ctx'=64] {'dp','ctx'}, use_global_device_ids=true, to_apply=%region_8.9 | all-reduce | flops 256 | bytes 2048 | tf_op jit(solution)/shard_map/psum | solution.py:197
  (184 shorter events, 13.4 us)
Async XLA Ops:
  0.6 4.8 %copy-start.61 = (f32[128]{0:T(128)S(1)}, f32[128]{0:T(128)}, u32[]{:S(2)}) copy-start(f32[128]{0:T(128)} %param.12) | copy-start | bytes 1540
  3.9 1.8 copy-start.47
  4.1 2.1 copy-start.2
  6.5 7.1 %copy-start.8 = (bf16[2,128,8,128]{3,1,2,0:T(8,128)(2,1)}, bf16[2,128,8,128]{3,1,2,0:T(8,128)(2,1)S(1)}, u32[]{:S(2)}) copy-start(bf16[2,128,8,128]{3,1,2,0:T(8,128)(2,1)S(1)} %maximum_convert_fusion) | copy-start | bytes 1572868
  7.2 6.3 %copy-start.19 = (bf16[2,128,8,128]{1,3,2,0:T(8,128)(2,1)}, bf16[2,128,8,128]{1,3,2,0:T(8,128)(2,1)S(1)}, u32[]{:S(2)}) copy-start(bf16[2,128,8,128]{1,3,2,0:T(8,128)(2,1)S(1)} %copy.223) | copy-start | bytes 1572868
  7.5 6.1 %copy-start.21 = (bf16[2,128,1024]{1,2,0:T(8,128)(2,1)}, bf16[2,128,1024]{1,2,0:T(8,128)(2,1)S(1)}, u32[]{:S(2)}) copy-start(bf16[2,128,1024]{1,2,0:T(8,128)(2,1)S(1)} %copy.224) | copy-start | bytes 1572868
  8.4 17.0 %collective-permute-start.1 = (bf16[2,128,1024]{1,2,0:T(8,128)(2,1)}, bf16[2,128,1024]{1,2,0:T(8,128)(2,1)}, u32[]{:S(2)}, u32[]{:S(2)}) collective-permute-start(bf16[2,128,1024]{1,2,0:T(8,128)(2,1)} %fusion.65), channel_id=1, source_target_pairs={{1,0},{2,1},{3,2},{4,3},{5,4},{6,5},{7,6},{8,7},{9,8},{10,9},{11,1... | collective-permute-start | bytes 1572872 | tf_op jit(solution)/shard_map/ppermute | solution.py:16
  13.6 2.3 copy-start.59
  21.4 3.1 %copy-start.63 = (pred[2]{0:T(512)(128)(4,1)S(1)}, pred[2]{0:T(512)(128)(4,1)}, u32[]{:S(2)}) copy-start(pred[2]{0:T(512)(128)(4,1)} %get-tuple-element.78) | copy-start | bytes 10
  21.4 3.1 %copy-start.64 = (pred[2]{0:T(512)(128)(4,1)S(1)}, pred[2]{0:T(512)(128)(4,1)}, u32[]{:S(2)}) copy-start(pred[2]{0:T(512)(128)(4,1)} %get-tuple-element.79) | copy-start | bytes 10
  21.4 3.1 %copy-start.65 = (pred[2]{0:T(512)(128)(4,1)S(1)}, pred[2]{0:T(512)(128)(4,1)}, u32[]{:S(2)}) copy-start(pred[2]{0:T(512)(128)(4,1)} %get-tuple-element.80) | copy-start | bytes 10
  21.4 3.1 %copy-start.66 = (pred[2]{0:T(512)(128)(4,1)S(1)}, pred[2]{0:T(512)(128)(4,1)}, u32[]{:S(2)}) copy-start(pred[2]{0:T(512)(128)(4,1)} %get-tuple-element.81) | copy-start | bytes 10
  21.4 3.1 %copy-start.67 = (s32[2]{0:T(128)S(1)}, s32[2]{0:T(128)}, u32[]{:S(2)}) copy-start(s32[2]{0:T(128)} %get-tuple-element.46) | copy-start | bytes 28
  21.4 3.1 %copy-start.68 = (s32[2]{0:T(128)S(1)}, s32[2]{0:T(128)}, u32[]{:S(2)}) copy-start(s32[2]{0:T(128)} %get-tuple-element.73) | copy-start | bytes 28
  21.4 3.1 %copy-start.69 = (s32[2]{0:T(128)S(1)}, s32[2]{0:T(128)}, u32[]{:S(2)}) copy-start(s32[2]{0:T(128)} %get-tuple-element.75) | copy-start | bytes 28
  21.4 3.1 %copy-start.70 = (s32[2]{0:T(128)S(1)}, s32[2]{0:T(128)}, u32[]{:S(2)}) copy-start(s32[2]{0:T(128)} %get-tuple-element.77) | copy-start | bytes 28
  21.5 3.1 %copy-start.58 = (s32[2,128]{1,0:T(2,128)S(1)}, s32[2,128]{1,0:T(2,128)}, u32[]{:S(2)}) copy-start(s32[2,128]{1,0:T(2,128)} %get-tuple-element.51) | copy-start | bytes 3076
  21.5 3.1 %copy-start.71 = (s32[2,128]{1,0:T(2,128)S(1)}, s32[2,128]{1,0:T(2,128)}, u32[]{:S(2)}) copy-start(s32[2,128]{1,0:T(2,128)} %param.10) | copy-start | bytes 3076
  21.5 3.9 %copy-start.20 = (bf16[2,128,8,128]{1,3,2,0:T(8,128)(2,1)S(1)}, bf16[2,128,8,128]{1,3,2,0:T(8,128)(2,1)}, u32[]{:S(2)}) copy-start(bf16[2,128,8,128]{1,3,2,0:T(8,128)(2,1)} %copy-done.19) | copy-start | bytes 1572868
  21.5 3.9 %copy-start.22 = (bf16[2,128,1024]{1,2,0:T(8,128)(2,1)S(1)}, bf16[2,128,1024]{1,2,0:T(8,128)(2,1)}, u32[]{:S(2)}) copy-start(bf16[2,128,1024]{1,2,0:T(8,128)(2,1)} %copy-done.21) | copy-start | bytes 1572868
  24.4 5.0 %copy-start.9 = (bf16[2,128,8,128]{3,1,2,0:T(8,128)(2,1)S(1)}, bf16[2,128,8,128]{3,1,2,0:T(8,128)(2,1)}, u32[]{:S(2)}) copy-start(bf16[2,128,8,128]{3,1,2,0:T(8,128)(2,1)} %copy-done.8) | copy-start | bytes 1572868
  25.4 6.4 %copy-start.49 = (pred[2,128,128]{1,2,0:T(8,128)(4,1)}, pred[2,128,128]{1,2,0:T(8,128)(4,1)S(1)}, u32[]{:S(2)}) copy-start(pred[2,128,128]{1,2,0:T(8,128)(4,1)S(1)} %get-tuple-element.68) | copy-start | bytes 98308
  27.5 14.6 %collective-permute-start = (bf16[2,128,1024]{1,2,0:T(8,128)(2,1)}, bf16[2,128,1024]{1,2,0:T(8,128)(2,1)}, u32[]{:S(2)}, u32[]{:S(2)}) collective-permute-start(bf16[2,128,1024]{1,2,0:T(8,128)(2,1)} %get-tuple-element.49), channel_id=1, source_target_pairs={{0,1},{1,2},{2,3},{3,4},{4,5},{5,6},{6,7},{7,8},{8,9},{9,10},{10,1... | collective-permute-start | bytes 1572872 | tf_op jit(solution)/shard_map/ppermute | solution.py:16
  31.8 14.9 %collective-permute-start.3 = (bf16[2,128,1024]{1,2,0:T(8,128)(2,1)}, bf16[2,128,1024]{1,2,0:T(8,128)(2,1)}, u32[]{:S(2)}, u32[]{:S(2)}) collective-permute-start(bf16[2,128,1024]{1,2,0:T(8,128)(2,1)} %get-tuple-element.48), channel_id=1, source_target_pairs={{1,0},{2,1},{3,2},{4,3},{5,4},{6,5},{7,6},{8,7},{9,8},{10,9},{11,1... | collective-permute-start | bytes 1572872 | tf_op jit(solution)/shard_map/ppermute | solution.py:16
  42.1 4.0 %copy-start.43 = (pred[2,128,128]{1,2,0:T(8,128)(4,1)S(1)}, pred[2,128,128]{1,2,0:T(8,128)(4,1)}, u32[]{:S(2)}) copy-start(pred[2,128,128]{1,2,0:T(8,128)(4,1)} %get-tuple-element.70) | copy-start | bytes 98308
  42.1 8.9 %collective-permute-start.2 = (bf16[2,128,1024]{1,2,0:T(8,128)(2,1)}, bf16[2,128,1024]{1,2,0:T(8,128)(2,1)S(1)}, u32[]{:S(2)}, u32[]{:S(2)}) collective-permute-start(bf16[2,128,1024]{1,2,0:T(8,128)(2,1)} %collective-permute-done), channel_id=1, source_target_pairs={{0,1},{1,2},{2,3},{3,4},{4,5},{5,6},{6,7},{7,8},{8,9},{9,10},{10,1... | collective-permute-start | bytes 1572872 | tf_op jit(solution)/shard_map/ppermute | solution.py:16
  46.0 2.2 copy-start.17
  46.1 2.2 copy-start.34
  46.7 2.0 copy-start.11
  48.7 2.4 %copy-start.45 = (pred[2,128,128]{1,2,0:T(8,128)(4,1)S(1)}, pred[2,128,128]{1,2,0:T(8,128)(4,1)}, u32[]{:S(2)}) copy-start(pred[2,128,128]{1,2,0:T(8,128)(4,1)} %get-tuple-element.69) | copy-start | bytes 98308
  51.8 2.4 %copy-start.29 = (f32[2,8,128,128,2]{3,2,4,1,0:T(8,128)S(1)}, f32[2,8,128,128,2]{3,2,4,1,0:T(8,128)}, u32[]{:S(2)}) copy-start(f32[2,8,128,128,2]{3,2,4,1,0:T(8,128)} %get-tuple-element.87) | copy-start | bytes 6291460
  51.8 2.4 %copy-start.41 = (bf16[2,128,8,128,1]{3,2,1,0,4:T(8,128)(2,1)S(1)}, bf16[2,128,8,128,1]{3,2,1,0,4:T(8,128)(2,1)}, u32[]{:S(2)}) copy-start(bf16[2,128,8,128,1]{3,2,1,0,4:T(8,128)(2,1)} %bitcast_bitcast_fusion) | copy-start | bytes 1572868
  51.8 2.4 %copy-start.50 = (pred[2,128,128]{1,2,0:T(8,128)(4,1)S(1)}, pred[2,128,128]{1,2,0:T(8,128)(4,1)}, u32[]{:S(2)}) copy-start(pred[2,128,128]{1,2,0:T(8,128)(4,1)} %copy-done.49) | copy-start | bytes 98308
  53.1 3.5 %copy-start.56 = (f32[2,2,8,128]{3,2,1,0:T(8,128)}, f32[2,2,8,128]{3,2,1,0:T(8,128)S(1)}, u32[]{:S(2)}) copy-start(f32[2,2,8,128]{3,2,1,0:T(8,128)S(1)} %add_add_fusion.2) | copy-start | bytes 49156
  68.0 2.6 %copy-start.14 = (f32[2,8,128,128,2]{3,2,4,1,0:T(8,128)S(1)}, f32[2,8,128,128,2]{3,2,4,1,0:T(8,128)}, u32[]{:S(2)}) copy-start(f32[2,8,128,128,2]{3,2,4,1,0:T(8,128)} %copy-done.13) | copy-start | bytes 6291460
  68.0 2.6 %copy-start.37 = (bf16[2,1,128,1024]{2,3,1,0:T(8,128)(2,1)S(1)}, bf16[2,1,128,1024]{2,3,1,0:T(8,128)(2,1)}, u32[]{:S(2)}) copy-start(bf16[2,1,128,1024]{2,3,1,0:T(8,128)(2,1)} %copy-done.36) | copy-start | bytes 1572868
  68.0 3.0 %copy-start.38 = (bf16[2,128,8,2,128]{1,4,3,2,0:T(8,128)(2,1)S(1)}, bf16[2,128,8,2,128]{1,4,3,2,0:T(8,128)(2,1)}, u32[]{:S(2)}) copy-start(bf16[2,128,8,2,128]{1,4,3,2,0:T(8,128)(2,1)} %copy.247) | copy-start | bytes 3145732
  68.0 3.0 %copy-start.46 = (pred[2,128,128]{1,2,0:T(8,128)(4,1)S(1)}, pred[2,128,128]{1,2,0:T(8,128)(4,1)}, u32[]{:S(2)}) copy-start(pred[2,128,128]{1,2,0:T(8,128)(4,1)} %get-tuple-element.69) | copy-start | bytes 98308
  68.0 3.0 %copy-start.55 = (f32[2,8,2,128]{3,2,1,0:T(2,128)S(1)}, f32[2,8,2,128]{3,2,1,0:T(2,128)}, u32[]{:S(2)}) copy-start(f32[2,8,2,128]{3,2,1,0:T(2,128)} %copy.286) | copy-start | bytes 49156
  68.1 3.0 %copy-start.57 = (f32[2,2,8,128]{3,2,1,0:T(8,128)S(1)}, f32[2,2,8,128]{3,2,1,0:T(8,128)}, u32[]{:S(2)}) copy-start(f32[2,2,8,128]{3,2,1,0:T(8,128)} %copy-done.56) | copy-start | bytes 49156
  75.1 3.1 %copy-start.26 = (bf16[2,8,2,128,128]{3,4,2,1,0:T(8,128)(2,1)}, bf16[2,8,2,128,128]{3,4,2,1,0:T(8,128)(2,1)S(1)}, u32[]{:S(2)}) copy-start(bf16[2,8,2,128,128]{3,4,2,1,0:T(8,128)(2,1)S(1)} %fusion.5) | copy-start | bytes 3145732
  75.6 2.2 copy-start.18
  75.7 2.5 %copy-start.10 = (bf16[2,128,8,128]{3,1,2,0:T(8,128)(2,1)S(1)}, bf16[2,128,8,128]{3,1,2,0:T(8,128)(2,1)}, u32[]{:S(2)}) copy-start(bf16[2,128,8,128]{3,1,2,0:T(8,128)(2,1)} %copy-done.8) | copy-start | bytes 1572868
  75.7 16.9 %collective-permute-start.5 = (f32[2,128,1024]{1,2,0:T(8,128)S(1)}, f32[2,128,1024]{1,2,0:T(8,128)S(1)}, u32[]{:S(2)}, u32[]{:S(2)}) collective-permute-start(f32[2,128,1024]{1,2,0:T(8,128)S(1)} %fusion.44), channel_id=1, source_target_pairs={{1,0},{2,1},{3,2},{4,3},{5,4},{6,5},{7,6},{8,7},{9,8},{10,9},{11,1... | collective-permute-start | bytes 3145736 | tf_op jit(solution)/shard_map/ppermute | solution.py:16
  79.8 12.9 %copy-start.6 = (f32[2,8,128,128,1]{3,2,4,1,0:T(8,128)}, f32[2,8,128,128,1]{3,2,4,1,0:T(8,128)S(1)}, u32[]{:S(2)}) copy-start(f32[2,8,128,128,1]{3,2,4,1,0:T(8,128)S(1)} %fusion.88) | copy-start | bytes 3145732
  80.8 13.3 %copy-start.27 = (f32[2,8,128,128,1]{2,3,4,1,0:T(8,128)}, f32[2,8,128,128,1]{2,3,4,1,0:T(8,128)S(1)}, u32[]{:S(2)}) copy-start(f32[2,8,128,128,1]{2,3,4,1,0:T(8,128)S(1)} %fusion.47) | copy-start | bytes 3145732
  94.1 17.3 %collective-permute-start.4 = (f32[2,128,1024]{1,2,0:T(8,128)}, f32[2,128,1024]{1,2,0:T(8,128)}, u32[]{:S(2)}, u32[]{:S(2)}) collective-permute-start(f32[2,128,1024]{1,2,0:T(8,128)} %get-tuple-element.45), channel_id=1, source_target_pairs={{0,1},{1,2},{2,3},{3,4},{4,5},{5,6},{6,7},{7,8},{8,9},{9,10},{10,1... | collective-permute-start | bytes 3145736 | tf_op jit(solution)/shard_map/ppermute | solution.py:16
  96.0 16.4 %collective-permute-start.6 = (f32[2,128,1024]{1,2,0:T(8,128)}, f32[2,128,1024]{1,2,0:T(8,128)}, u32[]{:S(2)}, u32[]{:S(2)}) collective-permute-start(f32[2,128,1024]{1,2,0:T(8,128)} %get-tuple-element.44), channel_id=1, source_target_pairs={{1,0},{2,1},{3,2},{4,3},{5,4},{6,5},{7,6},{8,7},{9,8},{10,9},{11,1... | collective-permute-start | bytes 3145736 | tf_op jit(solution)/shard_map/ppermute | solution.py:16
  107.7 1.9 copy-start.31
  107.7 2.2 copy-start.39
  109.8 2.6 %copy-start.4 = (f32[2,8,128,128,1]{3,2,4,1,0:T(8,128)}, f32[2,8,128,128,1]{3,2,4,1,0:T(8,128)S(1)}, u32[]{:S(2)}) copy-start(f32[2,8,128,128,1]{3,2,4,1,0:T(8,128)S(1)} %fusion.89) | copy-start | bytes 3145732
  109.8 2.6 %copy-start.7 = (f32[2,8,128,128,1]{3,2,4,1,0:T(8,128)S(1)}, f32[2,8,128,128,1]{3,2,4,1,0:T(8,128)}, u32[]{:S(2)}) copy-start(f32[2,8,128,128,1]{3,2,4,1,0:T(8,128)} %copy-done.6) | copy-start | bytes 3145732
  109.8 2.6 %copy-start.28 = (f32[2,8,128,128,1]{2,3,4,1,0:T(8,128)S(1)}, f32[2,8,128,128,1]{2,3,4,1,0:T(8,128)}, u32[]{:S(2)}) copy-start(f32[2,8,128,128,1]{2,3,4,1,0:T(8,128)} %copy-done.27) | copy-start | bytes 3145732
  111.3 4.2 %copy-start.25 = (f32[2,8,128,128,1]{2,3,4,1,0:T(8,128)}, f32[2,8,128,128,1]{2,3,4,1,0:T(8,128)S(1)}, u32[]{:S(2)}) copy-start(f32[2,8,128,128,1]{2,3,4,1,0:T(8,128)S(1)} %fusion.45) | copy-start | bytes 3145732
  112.4 5.1 %copy-start.15 = (f32[2,128,16,64]{3,2,1,0:T(8,128)S(1)}, f32[2,128,16,64]{3,2,1,0:T(8,128)}, u32[]{:S(2)}) copy-start(f32[2,128,16,64]{3,2,1,0:T(8,128)} %copy.325) | copy-start | bytes 3145732
  112.5 5.1 %copy-start.16 = (f32[2,128,16,64]{3,2,1,0:T(8,128)S(1)}, f32[2,128,16,64]{3,2,1,0:T(8,128)}, u32[]{:S(2)}) copy-start(f32[2,128,16,64]{3,2,1,0:T(8,128)} %copy.326) | copy-start | bytes 3145732
  115.5 2.7 %copy-start.60 = (f32[128]{0:T(128)S(1)}, f32[128]{0:T(128)}, u32[]{:S(2)}) copy-start(f32[128]{0:T(128)} %param.11) | copy-start | bytes 1540
  115.5 18.2 %collective-permute-start.7 = (f32[2,128,1024]{1,2,0:T(8,128)}, f32[2,128,1024]{1,2,0:T(8,128)}, u32[]{:S(2)}, u32[]{:S(2)}) collective-permute-start(f32[2,128,1024]{1,2,0:T(8,128)} %get-tuple-element.43), channel_id=1, source_target_pairs={{0,1},{1,2},{2,3},{3,4},{4,5},{5,6},{6,7},{7,8},{8,9},{9,10},{10,1... | collective-permute-start | bytes 3145736 | tf_op jit(solution)/shard_map/ppermute | solution.py:16
  118.2 2.5 %copy-start = (f32[2,128,16,64]{3,2,1,0:T(8,128)}, f32[2,128,16,64]{3,2,1,0:T(8,128)S(1)}, u32[]{:S(2)}) copy-start(f32[2,128,16,64]{3,2,1,0:T(8,128)S(1)} %get-tuple-element.52) | copy-start | bytes 3145732
  118.2 2.5 %copy-start.1 = (f32[2,128,16,64]{3,2,1,0:T(8,128)}, f32[2,128,16,64]{3,2,1,0:T(8,128)S(1)}, u32[]{:S(2)}) copy-start(f32[2,128,16,64]{3,2,1,0:T(8,128)S(1)} %get-tuple-element.53) | copy-start | bytes 3145732
  129.9 2.4 %copy-start.40 = (bf16[2,128,8,2,128]{1,4,3,2,0:T(8,128)(2,1)S(1)}, bf16[2,128,8,2,128]{1,4,3,2,0:T(8,128)(2,1)}, u32[]{:S(2)}) copy-start(bf16[2,128,8,2,128]{1,4,3,2,0:T(8,128)(2,1)} %get-tuple-element.91) | copy-start | bytes 3145732
  129.9 3.8 %copy-start.5 = (f32[2,8,128,128,1]{3,2,4,1,0:T(8,128)S(1)}, f32[2,8,128,128,1]{3,2,4,1,0:T(8,128)}, u32[]{:S(2)}) copy-start(f32[2,8,128,128,1]{3,2,4,1,0:T(8,128)} %copy-done.4) | copy-start | bytes 3145732
  136.2 1.7 copy-start.32
  141.5 2.3 copy-start.72
  (17 other events, 23.6 us)
where the time goes:
time: 236 us; the launch traced here: 235 us
  blocking collectives  91 us (39%)
  local copies, waits for them, and re-layouts  45.8 us (19%)
  other arithmetic  40.8 us (17%)
  starting transfers between devices  22.5 us (10%)
  matrix products  17.9 us (8%)
  waiting for transfers between devices  15.2 us (6%)
    psum x1, blocking collectives, shards(): lax.psum((grad_gain_q, grad_gain_k), ('dp', 'ctx'))  91 us
    unnamed x158, local copies, waits for them, and re-layouts  24.7 us
    ppermute x8, starting transfers between devices, from_behind(): return lax.ppermute(block, axis, route)  22.5 us
    ppermute x8, waiting for transfers between devices, from_behind(): return lax.ppermute(block, axis, route)  15.2 us
    reshape x2, local copies, waits for them, and re-layouts, shards(): cotangent_heads = cotangent.reshape(2, block, kv_heads, repeat, head_width)  6.23 us
    unnamed x1, other arithmetic  5.11 us
    convert_element_type x1, other arithmetic, shards(): grad_queries.reshape(2, block, -1).astype(jnp.bfloat16)  4.83 us
  transfers between devices with their start and end apart: 8, of which 3 were waited for; matrix products, arithmetic and copies ran while one was open for 23% of the time, Pallas kernels for 0%

commit v1 on v0

--- a/solution.py
+++ b/solution.py
@@ -194,7 +194,7 @@
     grad_v_flat = key_value_gradient[:, 1]
     grad_queries, grad_gain_q = q_back(grad_q_heads.reshape(2, block, q_heads, head_width))
     grad_keys, grad_gain_k = k_back(grad_k_heads)
-    grad_gain_q, grad_gain_k = lax.psum((grad_gain_q, grad_gain_k), ("dp", "ctx"))
+    grad_gain_q, grad_gain_k = lax.psum(lax.psum((grad_gain_q, grad_gain_k), "ctx"), "dp")
     return (
         attended_heads.reshape(2, block, -1),
         grad_queries.reshape(2, block, -1).astype(jnp.bfloat16),

time: 236 us -> 294 us (1.25)
  the two profiles are of different devices: /device:TPU:1 before, /device:TPU:128 now
where the time goes in v1:
time: 294 us; the launch traced here: 293 us
  blocking collectives  138 us (47%)
  local copies, waits for them, and re-layouts  45.8 us (16%)
  other arithmetic  40.7 us (14%)
  starting transfers between devices  28.3 us (10%)
  waiting for transfers between devices  19.8 us (7%)
  matrix products  17.9 us (6%)
    psum x1, blocking collectives, shards(): lax.psum((grad_gain_q, grad_gain_k), 'ctx')  127 us
    ppermute x8, starting transfers between devices, from_behind(): return lax.ppermute(block, axis, route)  28.3 us
    unnamed x158, local copies, waits for them, and re-layouts  24.7 us
    ppermute x8, waiting for transfers between devices, from_behind(): return lax.ppermute(block, axis, route)  19.8 us
    psum x1, blocking collectives, shards(): lax.psum(lax.psum((grad_gain_q, grad_gain_k), 'ctx'), 'dp')  11 us
    reshape x2, local copies, waits for them, and re-layouts, shards(): cotangent_heads = cotangent.reshape(2, block, kv_heads, repeat, head_width)  6.24 us
  transfers between devices with their start and end apart: 8, of which 4 were waited for; matrix products, arithmetic and copies ran while one was open for 19% of the time, Pallas kernels for 0%

profile of v1, /device:TPU:128, one launch (start us, length us, event | category | flops | bytes accessed | tf_op | source)
XLA Modules:
  0.0 292.6 jit_solution(697410935277196893)
XLA Ops:
  2.4 1.3 copy.215
  4.1 0.7 fusion.83
  7.5 0.9 fusion.65
  8.4 3.9 %collective-permute-start.1 = (bf16[2,128,1024]{1,2,0:T(8,128)(2,1)}, bf16[2,128,1024]{1,2,0:T(8,128)(2,1)}, u32[]{:S(2)}, u32[]{:S(2)}) collective-permute-start(bf16[2,128,1024]{1,2,0:T(8,128)(2,1)} %fusion.65), channel_id=1, source_target_pairs={{1,0},{2,1},{3,2},{4,3},{5,4},{6,5},{7,6},{8,7},{9,8},{10,9},{11,1... | collective-permute-start | bytes 1572872 | tf_op jit(solution)/shard_map/ppermute | solution.py:16
  12.3 1.5 copy.330
  14.6 0.7 fusion.21
  15.4 0.7 multiply_subtract_fusion
  16.1 2.0 copy.219
  18.0 2.0 copy.220
  20.2 2.9 fusion.3
  23.3 0.8 compare_and_fusion.2
  24.2 2.1 broadcast_select_fusion
  26.2 1.9 collective-permute-start
  28.2 2.4 fusion.15
  30.6 7.0 %collective-permute-start.3 = (bf16[2,128,1024]{1,2,0:T(8,128)(2,1)}, bf16[2,128,1024]{1,2,0:T(8,128)(2,1)}, u32[]{:S(2)}, u32[]{:S(2)}) collective-permute-start(bf16[2,128,1024]{1,2,0:T(8,128)(2,1)} %get-tuple-element.50), channel_id=1, source_target_pairs={{1,0},{2,1},{3,2},{4,3},{5,4},{6,5},{7,6},{8,7},{9,8},{10,9},{11,1... | collective-permute-start | bytes 1572872 | tf_op jit(solution)/shard_map/ppermute | solution.py:16
  37.5 0.8 bitcast_bitcast_fusion
  38.4 2.6 reshape.655
  40.9 3.7 %copy.247 = bf16[2,128,8,2,128]{1,4,3,2,0:T(8,128)(2,1)} copy(bf16[2,128,8,2,128]{4,3,2,1,0:T(2,128)(2,1)} %reshape.655) | data formatting | bytes 2097152 | tf_op jit(solution)/shard_map/reshape | solution.py:132
  44.6 2.2 collective-permute-start.2
  46.8 1.3 pad_maximum_fusion.5
  48.8 1.5 select_bitcast_fusion
  50.8 8.0 %collective-permute-done.2 = bf16[2,128,1024]{1,2,0:T(8,128)(2,1)S(1)} collective-permute-done((bf16[2,128,1024]{1,2,0:T(8,128)(2,1)}, bf16[2,128,1024]{1,2,0:T(8,128)(2,1)S(1)}, u32[]{:S(2)}, u32[]{:S(2)}) %collective-permute-start.2) | collective-permute-done | bytes 524320 | tf_op jit(solution)/shard_map/ppermute | solution.py:16
  60.0 0.8 copy-done.13
  60.9 1.0 copy-done.29
  62.0 2.4 bitcast_convert_fusion
  64.3 4.2 %copy.285 = f32[2,8,2,128,128]{4,2,1,3,0:T(2,128)} copy(f32[2,8,2,128,128]{3,4,2,1,0:T(8,128)} %get-tuple-element.92) | data formatting | bytes 4194304
  68.5 5.1 %multiply_reduce_fusion = f32[2,8,2,128]{2,1,3,0:T(8,128)} fusion(f32[2,8,2,128,128]{4,2,1,3,0:T(2,128)} %copy.285, bf16[2,128,8,2,128]{4,3,2,1,0:T(2,128)(2,1)} %reshape.655), kind=kLoop, calls=%fused_computation.40 | loop fusion | flops 1568768 | bytes 3162112
  73.6 2.2 copy.286
  75.8 2.5 fusion.49
  78.8 0.8 fusion.9
  79.6 0.8 copy-done.12
  80.5 0.8 fusion.7
  81.2 0.8 copy-done.30
  82.1 0.7 fusion.5
  83.5 2.1 collective-permute-start.5
  88.5 9.3 %collective-permute-done.5 = f32[2,128,1024]{1,2,0:T(8,128)S(1)} collective-permute-done((f32[2,128,1024]{1,2,0:T(8,128)S(1)}, f32[2,128,1024]{1,2,0:T(8,128)S(1)}, u32[]{:S(2)}, u32[]{:S(2)}) %collective-permute-start.5) | collective-permute-done | bytes 1048608 | tf_op jit(solution)/shard_map/ppermute | solution.py:16
  97.8 1.5 fusion.43
  99.3 1.9 collective-permute-start.4
  101.2 7.4 %collective-permute-start.6 = (f32[2,128,1024]{1,2,0:T(8,128)}, f32[2,128,1024]{1,2,0:T(8,128)}, u32[]{:S(2)}, u32[]{:S(2)}) collective-permute-start(f32[2,128,1024]{1,2,0:T(8,128)} %get-tuple-element.46), channel_id=1, source_target_pairs={{1,0},{2,1},{3,2},{4,3},{5,4},{6,5},{7,6},{8,7},{9,8},{10,9},{11,1... | collective-permute-start | bytes 3145736 | tf_op jit(solution)/shard_map/ppermute | solution.py:16
  108.6 1.5 fusion.84
  110.1 3.3 %copy.325 = f32[2,128,16,64]{3,2,1,0:T(8,128)} copy(f32[2,128,16,64]{1,3,2,0:T(8,128)} %get-tuple-element.60) | data formatting | bytes 2097152
  113.4 3.3 %copy.326 = f32[2,128,16,64]{3,2,1,0:T(8,128)} copy(f32[2,128,16,64]{1,3,2,0:T(8,128)} %get-tuple-element.61) | data formatting | bytes 2097152
  116.7 1.9 fusion.89
  118.8 1.5 fusion.45
  121.0 3.0 %fusion.32 = (f32[1,2,128,1024]{2,3,1,0:T(8,128)S(1)}, f32[2,128,1024]{1,2,0:T(8,128)}) fusion(f32[2,1,128,1024]{2,3,1,0:T(8,128)S(1)} %bitcast.301, f32[2,1,128,1024]{2,3,1,0:T(8,128)S(1)} %bitcast.319, f32[2,128,1024]{1,2,0:T(8,128)} %collective-permute-done.6, pred[]{:T(512)S(6)} %eq.6, f32[2,1,128,1024]{2,3,1,0:T(8,128)S(1)} %bitcast.323, ...), kind=kLoop, calls=%fused_computation.63 | loop fusion | flops 1572864 | bytes 8388610 | tf_op jit(solution)/shard_map/stack | solution.py:192
  124.0 2.0 collective-permute-start.7
  126.7 2.5 multiply_reduce_fusion.1
  129.2 1.6 copy.242
  130.8 1.3 multiply_multiply_fusion.1
  132.2 1.5 copy.243
  133.6 4.8 %fusion = bf16[2,128,16,128]{3,2,1,0:T(8,128)(2,1)} fusion(f32[2,128,16]{2,1,0:T(8,128)} %copy.243, f32[128]{0:T(128)} %param.11, f32[2,128,16]{2,1,0:T(8,128)S(1)} %copy.218, f32[2,128,16,64]{3,2,1,0:T(8,128)} %copy-done.1, f32[2,128,16,64]{3,2,1,0:T(8,128)} %copy-done, f32[2,128,16,128]{3,2,1,0:T(8,128)S(1)} %bitcast.300), kind=kLoop, calls=%fused_computation.1 | loop fusion | flops 3670016 | bytes 5276160 | tf_op jit(solution)/shard_map/convert_element_type | solution.py:200
  138.5 2.4 convert_element_type.84
  140.9 1.3 copy.267
  142.2 1.9 collective-permute-done.7
  144.1 1.5 fusion.41
  145.7 0.9 fusion.64
  147.0 1.4 copy.328
  148.4 1.0 copy.269
  149.4 1.6 multiply_add_fusion.4
  151.0 0.9 multiply_reduce_fusion.2
  151.9 1.0 fusion.22
  153.2 1.0 copy.268
  154.3 127.4 %all-reduce.4 = (f32[128]{0:T(128)S(1)}, f32[128]{0:T(128)S(1)}) all-reduce(f32[128]{0:T(128)S(1)} %copy-done.72, f32[128]{0:T(128)S(1)} %get-tuple-element.38), channel_id=1, replica_groups=mesh['dp'=4,'ctx'=64] {'ctx'}, use_global_device_ids=true, to_apply=%region_8.9 | all-reduce | flops 256 | bytes 2048 | tf_op jit(solution)/shard_map/psum | solution.py:197
  281.6 11.0 %all-reduce.5 = (f32[128]{0:T(128)}, f32[128]{0:T(128)}) all-reduce(f32[128]{0:T(128)S(1)} %get-tuple-element.40, f32[128]{0:T(128)S(1)} %get-tuple-element.41), channel_id=1, replica_groups=mesh['dp'=4,'ctx'=64] {'dp'}, use_global_device_ids=true, to_apply=%region_9.10 | all-reduce | flops 256 | bytes 2048 | tf_op jit(solution)/shard_map/psum | solution.py:197
  (185 shorter events, 14.6 us)
Async XLA Ops:
  0.6 4.7 %copy-start.61 = (f32[128]{0:T(128)S(1)}, f32[128]{0:T(128)}, u32[]{:S(2)}) copy-start(f32[128]{0:T(128)} %param.12) | copy-start | bytes 1540
  3.8 1.9 copy-start.47
  4.1 2.1 copy-start.2
  6.5 5.8 %copy-start.8 = (bf16[2,128,8,128]{3,1,2,0:T(8,128)(2,1)}, bf16[2,128,8,128]{3,1,2,0:T(8,128)(2,1)S(1)}, u32[]{:S(2)}) copy-start(bf16[2,128,8,128]{3,1,2,0:T(8,128)(2,1)S(1)} %maximum_convert_fusion) | copy-start | bytes 1572868
  7.2 5.1 %copy-start.19 = (bf16[2,128,8,128]{1,3,2,0:T(8,128)(2,1)}, bf16[2,128,8,128]{1,3,2,0:T(8,128)(2,1)S(1)}, u32[]{:S(2)}) copy-start(bf16[2,128,8,128]{1,3,2,0:T(8,128)(2,1)S(1)} %copy.223) | copy-start | bytes 1572868
  7.5 4.8 %copy-start.21 = (bf16[2,128,1024]{1,2,0:T(8,128)(2,1)}, bf16[2,128,1024]{1,2,0:T(8,128)(2,1)S(1)}, u32[]{:S(2)}) copy-start(bf16[2,128,1024]{1,2,0:T(8,128)(2,1)S(1)} %copy.224) | copy-start | bytes 1572868
  8.4 15.8 %collective-permute-start.1 = (bf16[2,128,1024]{1,2,0:T(8,128)(2,1)}, bf16[2,128,1024]{1,2,0:T(8,128)(2,1)}, u32[]{:S(2)}, u32[]{:S(2)}) collective-permute-start(bf16[2,128,1024]{1,2,0:T(8,128)(2,1)} %fusion.65), channel_id=1, source_target_pairs={{1,0},{2,1},{3,2},{4,3},{5,4},{6,5},{7,6},{8,7},{9,8},{10,9},{11,1... | collective-permute-start | bytes 1572872 | tf_op jit(solution)/shard_map/ppermute | solution.py:16
  12.3 2.3 copy-start.59
  20.1 3.1 %copy-start.63 = (pred[2]{0:T(512)(128)(4,1)S(1)}, pred[2]{0:T(512)(128)(4,1)}, u32[]{:S(2)}) copy-start(pred[2]{0:T(512)(128)(4,1)} %get-tuple-element.80) | copy-start | bytes 10
  20.1 3.1 %copy-start.64 = (pred[2]{0:T(512)(128)(4,1)S(1)}, pred[2]{0:T(512)(128)(4,1)}, u32[]{:S(2)}) copy-start(pred[2]{0:T(512)(128)(4,1)} %get-tuple-element.81) | copy-start | bytes 10
  20.1 3.1 %copy-start.65 = (pred[2]{0:T(512)(128)(4,1)S(1)}, pred[2]{0:T(512)(128)(4,1)}, u32[]{:S(2)}) copy-start(pred[2]{0:T(512)(128)(4,1)} %get-tuple-element.82) | copy-start | bytes 10
  20.1 3.1 %copy-start.66 = (pred[2]{0:T(512)(128)(4,1)S(1)}, pred[2]{0:T(512)(128)(4,1)}, u32[]{:S(2)}) copy-start(pred[2]{0:T(512)(128)(4,1)} %get-tuple-element.83) | copy-start | bytes 10
  20.1 3.1 %copy-start.67 = (s32[2]{0:T(128)S(1)}, s32[2]{0:T(128)}, u32[]{:S(2)}) copy-start(s32[2]{0:T(128)} %get-tuple-element.48) | copy-start | bytes 28
  20.2 3.1 %copy-start.68 = (s32[2]{0:T(128)S(1)}, s32[2]{0:T(128)}, u32[]{:S(2)}) copy-start(s32[2]{0:T(128)} %get-tuple-element.75) | copy-start | bytes 28
  20.2 3.1 %copy-start.69 = (s32[2]{0:T(128)S(1)}, s32[2]{0:T(128)}, u32[]{:S(2)}) copy-start(s32[2]{0:T(128)} %get-tuple-element.77) | copy-start | bytes 28
  20.2 3.1 %copy-start.70 = (s32[2]{0:T(128)S(1)}, s32[2]{0:T(128)}, u32[]{:S(2)}) copy-start(s32[2]{0:T(128)} %get-tuple-element.79) | copy-start | bytes 28
  20.2 3.1 %copy-start.58 = (s32[2,128]{1,0:T(2,128)S(1)}, s32[2,128]{1,0:T(2,128)}, u32[]{:S(2)}) copy-start(s32[2,128]{1,0:T(2,128)} %get-tuple-element.53) | copy-start | bytes 3076
  20.2 3.1 %copy-start.71 = (s32[2,128]{1,0:T(2,128)S(1)}, s32[2,128]{1,0:T(2,128)}, u32[]{:S(2)}) copy-start(s32[2,128]{1,0:T(2,128)} %param.10) | copy-start | bytes 3076
  20.2 3.9 %copy-start.20 = (bf16[2,128,8,128]{1,3,2,0:T(8,128)(2,1)S(1)}, bf16[2,128,8,128]{1,3,2,0:T(8,128)(2,1)}, u32[]{:S(2)}) copy-start(bf16[2,128,8,128]{1,3,2,0:T(8,128)(2,1)} %copy-done.19) | copy-start | bytes 1572868
  20.2 3.9 %copy-start.22 = (bf16[2,128,1024]{1,2,0:T(8,128)(2,1)S(1)}, bf16[2,128,1024]{1,2,0:T(8,128)(2,1)}, u32[]{:S(2)}) copy-start(bf16[2,128,1024]{1,2,0:T(8,128)(2,1)} %copy-done.21) | copy-start | bytes 1572868
  23.2 5.0 %copy-start.9 = (bf16[2,128,8,128]{3,1,2,0:T(8,128)(2,1)S(1)}, bf16[2,128,8,128]{3,1,2,0:T(8,128)(2,1)}, u32[]{:S(2)}) copy-start(bf16[2,128,8,128]{3,1,2,0:T(8,128)(2,1)} %copy-done.8) | copy-start | bytes 1572868
  24.1 6.5 %copy-start.49 = (pred[2,128,128]{1,2,0:T(8,128)(4,1)}, pred[2,128,128]{1,2,0:T(8,128)(4,1)S(1)}, u32[]{:S(2)}) copy-start(pred[2,128,128]{1,2,0:T(8,128)(4,1)S(1)} %get-tuple-element.70) | copy-start | bytes 98308
  26.2 18.4 %collective-permute-start = (bf16[2,128,1024]{1,2,0:T(8,128)(2,1)}, bf16[2,128,1024]{1,2,0:T(8,128)(2,1)}, u32[]{:S(2)}, u32[]{:S(2)}) collective-permute-start(bf16[2,128,1024]{1,2,0:T(8,128)(2,1)} %get-tuple-element.51), channel_id=1, source_target_pairs={{0,1},{1,2},{2,3},{3,4},{4,5},{5,6},{6,7},{7,8},{8,9},{9,10},{10,1... | collective-permute-start | bytes 1572872 | tf_op jit(solution)/shard_map/ppermute | solution.py:16
  30.6 18.2 %collective-permute-start.3 = (bf16[2,128,1024]{1,2,0:T(8,128)(2,1)}, bf16[2,128,1024]{1,2,0:T(8,128)(2,1)}, u32[]{:S(2)}, u32[]{:S(2)}) collective-permute-start(bf16[2,128,1024]{1,2,0:T(8,128)(2,1)} %get-tuple-element.50), channel_id=1, source_target_pairs={{1,0},{2,1},{3,2},{4,3},{5,4},{6,5},{7,6},{8,7},{9,8},{10,9},{11,1... | collective-permute-start | bytes 1572872 | tf_op jit(solution)/shard_map/ppermute | solution.py:16
  44.6 3.5 %copy-start.43 = (pred[2,128,128]{1,2,0:T(8,128)(4,1)S(1)}, pred[2,128,128]{1,2,0:T(8,128)(4,1)}, u32[]{:S(2)}) copy-start(pred[2,128,128]{1,2,0:T(8,128)(4,1)} %get-tuple-element.72) | copy-start | bytes 98308
  44.6 14.2 %collective-permute-start.2 = (bf16[2,128,1024]{1,2,0:T(8,128)(2,1)}, bf16[2,128,1024]{1,2,0:T(8,128)(2,1)S(1)}, u32[]{:S(2)}, u32[]{:S(2)}) collective-permute-start(bf16[2,128,1024]{1,2,0:T(8,128)(2,1)} %collective-permute-done), channel_id=1, source_target_pairs={{0,1},{1,2},{2,3},{3,4},{4,5},{5,6},{6,7},{7,8},{8,9},{9,10},{10,1... | collective-permute-start | bytes 1572872 | tf_op jit(solution)/shard_map/ppermute | solution.py:16
  48.1 2.2 copy-start.17
  48.1 2.2 copy-start.34
  48.8 2.0 copy-start.11
  50.8 8.1 %copy-start.45 = (pred[2,128,128]{1,2,0:T(8,128)(4,1)S(1)}, pred[2,128,128]{1,2,0:T(8,128)(4,1)}, u32[]{:S(2)}) copy-start(pred[2,128,128]{1,2,0:T(8,128)(4,1)} %get-tuple-element.71) | copy-start | bytes 98308
  59.5 2.4 copy-start.29
  59.5 2.4 copy-start.41
  59.5 2.4 copy-start.50
  60.9 3.5 %copy-start.56 = (f32[2,2,8,128]{3,2,1,0:T(8,128)}, f32[2,2,8,128]{3,2,1,0:T(8,128)S(1)}, u32[]{:S(2)}) copy-start(f32[2,2,8,128]{3,2,1,0:T(8,128)S(1)} %add_add_fusion.2) | copy-start | bytes 49156
  75.8 2.6 copy-start.14
  75.8 2.6 copy-start.37
  75.8 3.0 %copy-start.38 = (bf16[2,128,8,2,128]{1,4,3,2,0:T(8,128)(2,1)S(1)}, bf16[2,128,8,2,128]{1,4,3,2,0:T(8,128)(2,1)}, u32[]{:S(2)}) copy-start(bf16[2,128,8,2,128]{1,4,3,2,0:T(8,128)(2,1)} %copy.247) | copy-start | bytes 3145732
  75.8 3.0 %copy-start.46 = (pred[2,128,128]{1,2,0:T(8,128)(4,1)S(1)}, pred[2,128,128]{1,2,0:T(8,128)(4,1)}, u32[]{:S(2)}) copy-start(pred[2,128,128]{1,2,0:T(8,128)(4,1)} %get-tuple-element.71) | copy-start | bytes 98308
  75.8 3.0 %copy-start.55 = (f32[2,8,2,128]{3,2,1,0:T(2,128)S(1)}, f32[2,8,2,128]{3,2,1,0:T(2,128)}, u32[]{:S(2)}) copy-start(f32[2,8,2,128]{3,2,1,0:T(2,128)} %copy.286) | copy-start | bytes 49156
  75.8 3.0 %copy-start.57 = (f32[2,2,8,128]{3,2,1,0:T(8,128)S(1)}, f32[2,2,8,128]{3,2,1,0:T(8,128)}, u32[]{:S(2)}) copy-start(f32[2,2,8,128]{3,2,1,0:T(8,128)} %copy-done.56) | copy-start | bytes 49156
  82.9 3.1 %copy-start.26 = (bf16[2,8,2,128,128]{3,4,2,1,0:T(8,128)(2,1)}, bf16[2,8,2,128,128]{3,4,2,1,0:T(8,128)(2,1)S(1)}, u32[]{:S(2)}) copy-start(bf16[2,8,2,128,128]{3,4,2,1,0:T(8,128)(2,1)S(1)} %fusion.5) | copy-start | bytes 3145732
  83.4 2.2 copy-start.18
  83.5 2.5 copy-start.10
  83.5 14.4 %collective-permute-start.5 = (f32[2,128,1024]{1,2,0:T(8,128)S(1)}, f32[2,128,1024]{1,2,0:T(8,128)S(1)}, u32[]{:S(2)}, u32[]{:S(2)}) collective-permute-start(f32[2,128,1024]{1,2,0:T(8,128)S(1)} %fusion.44), channel_id=1, source_target_pairs={{1,0},{2,1},{3,2},{4,3},{5,4},{6,5},{7,6},{8,7},{9,8},{10,9},{11,1... | collective-permute-start | bytes 3145736 | tf_op jit(solution)/shard_map/ppermute | solution.py:16
  87.5 10.3 %copy-start.6 = (f32[2,8,128,128,1]{3,2,4,1,0:T(8,128)}, f32[2,8,128,128,1]{3,2,4,1,0:T(8,128)S(1)}, u32[]{:S(2)}) copy-start(f32[2,8,128,128,1]{3,2,4,1,0:T(8,128)S(1)} %fusion.88) | copy-start | bytes 3145732
  88.5 10.8 %copy-start.27 = (f32[2,8,128,128,1]{2,3,4,1,0:T(8,128)}, f32[2,8,128,128,1]{2,3,4,1,0:T(8,128)S(1)}, u32[]{:S(2)}) copy-start(f32[2,8,128,128,1]{2,3,4,1,0:T(8,128)S(1)} %fusion.47) | copy-start | bytes 3145732
  99.3 21.1 %collective-permute-start.4 = (f32[2,128,1024]{1,2,0:T(8,128)}, f32[2,128,1024]{1,2,0:T(8,128)}, u32[]{:S(2)}, u32[]{:S(2)}) collective-permute-start(f32[2,128,1024]{1,2,0:T(8,128)} %get-tuple-element.47), channel_id=1, source_target_pairs={{0,1},{1,2},{2,3},{3,4},{4,5},{5,6},{6,7},{7,8},{8,9},{9,10},{10,1... | collective-permute-start | bytes 3145736 | tf_op jit(solution)/shard_map/ppermute | solution.py:16
  101.2 19.8 %collective-permute-start.6 = (f32[2,128,1024]{1,2,0:T(8,128)}, f32[2,128,1024]{1,2,0:T(8,128)}, u32[]{:S(2)}, u32[]{:S(2)}) collective-permute-start(f32[2,128,1024]{1,2,0:T(8,128)} %get-tuple-element.46), channel_id=1, source_target_pairs={{1,0},{2,1},{3,2},{4,3},{5,4},{6,5},{7,6},{8,7},{9,8},{10,9},{11,1... | collective-permute-start | bytes 3145736 | tf_op jit(solution)/shard_map/ppermute | solution.py:16
  116.7 1.9 copy-start.31
  116.7 2.2 copy-start.39
  118.8 2.1 copy-start.4
  118.8 2.1 copy-start.7
  118.8 2.1 copy-start.28
  120.3 3.7 %copy-start.25 = (f32[2,8,128,128,1]{2,3,4,1,0:T(8,128)}, f32[2,8,128,128,1]{2,3,4,1,0:T(8,128)S(1)}, u32[]{:S(2)}) copy-start(f32[2,8,128,128,1]{2,3,4,1,0:T(8,128)S(1)} %fusion.45) | copy-start | bytes 3145732
  121.0 5.1 %copy-start.15 = (f32[2,128,16,64]{3,2,1,0:T(8,128)S(1)}, f32[2,128,16,64]{3,2,1,0:T(8,128)}, u32[]{:S(2)}) copy-start(f32[2,128,16,64]{3,2,1,0:T(8,128)} %copy.325) | copy-start | bytes 3145732
  121.0 5.1 %copy-start.16 = (f32[2,128,16,64]{3,2,1,0:T(8,128)S(1)}, f32[2,128,16,64]{3,2,1,0:T(8,128)}, u32[]{:S(2)}) copy-start(f32[2,128,16,64]{3,2,1,0:T(8,128)} %copy.326) | copy-start | bytes 3145732
  124.0 2.7 copy-start.60
  124.0 20.1 %collective-permute-start.7 = (f32[2,128,1024]{1,2,0:T(8,128)}, f32[2,128,1024]{1,2,0:T(8,128)}, u32[]{:S(2)}, u32[]{:S(2)}) collective-permute-start(f32[2,128,1024]{1,2,0:T(8,128)} %get-tuple-element.45), channel_id=1, source_target_pairs={{0,1},{1,2},{2,3},{3,4},{4,5},{5,6},{6,7},{7,8},{8,9},{9,10},{10,1... | collective-permute-start | bytes 3145736 | tf_op jit(solution)/shard_map/ppermute | solution.py:16
  126.7 2.5 copy-start
  126.7 2.5 copy-start.1
  138.5 2.4 copy-start.40
  138.5 5.6 %copy-start.5 = (f32[2,8,128,128,1]{3,2,4,1,0:T(8,128)S(1)}, f32[2,8,128,128,1]{3,2,4,1,0:T(8,128)}, u32[]{:S(2)}) copy-start(f32[2,8,128,128,1]{3,2,4,1,0:T(8,128)} %copy-done.4) | copy-start | bytes 3145732
  146.6 1.7 copy-start.32
  151.9 2.3 copy-start.72
  (17 other events, 23.7 us)
